TPU v7x, 32 devices: a whole 2x2x4 slice. The times are simulated.
32 devices in a mesh: pert: 2 (over y), ga: 4 (over z), band: 4 (over x, core).
Axes of the slice: x: 2, y: 2, z: 4, core: 2. Of those that a mesh axis runs over, the one named last changes fastest.
Arguments:
- psi: float32 [2, 4, 131072], P(None, 'band', 'ga'), may hold values from -6 to 6
- potential: float32 [256, 128, 128], P('pert', 'ga'), parts along dimension 0, may hold values from 1 to 3
- miller: int32 [131072], replicated, may hold values from 0 to 2097151, as said below
- occupied: int32 [4], replicated, may hold values 0 or 1
Outputs:
- projected: float32 [2, 8, 131072], P(None, ('pert', 'band'), 'ga'), parts along dimension 1
There are 2 independent parts, one for each index of `pert`. A program takes and returns all parts, laid end to end along the dimension named above; an argument that names none is the same for every part. Nothing has to cross between parts.
Inputs may be any that keep to these rules, and one draw needn't show every extreme that they name: `miller`: entry k is the flat index a 128^2 + b * 128 + c of coefficient k, with Fourier indices a, b, c in 0..127 taken modulo 128; the entries are distinct; each of a, b, c, read as a signed index in -64..128/2-1, lies in -32..128/4-1; the j-th block of 32768 entries holds only points whose signed a plus 128/4 is congruent to j modulo 131072/32768.
All inputs are finite; a program needn't handle non-finite values.
Results may differ from a plain program's by a relative error of at most 0.00013.
Values sent between devices are 32-bit elements; how exact they have to be, the bound alone decides.
A program may use at most 64 MiB of HBM per device.

v0:
```python
import jax
import jax.numpy as jnp
from jax import lax
from jax.sharding import PartitionSpec as P

NPW = 131072
highest = lax.Precision.HIGHEST


def phases(first_index, second_index, direction, length):
    turns = first_index[:, None] * second_index[None, :] % length
    angle = direction * 2.0 * jnp.pi / length * turns.astype(jnp.float32)
    return (jnp.cos(angle), jnp.sin(angle))


def contract(pattern, real_part, imag_part, twiddle):
    cosine, sine_part = twiddle
    out_real = jnp.einsum(pattern, real_part, cosine, precision=highest) - jnp.einsum(
        pattern, imag_part, sine_part, precision=highest
    )
    out_imag = jnp.einsum(pattern, real_part, sine_part, precision=highest) + jnp.einsum(
        pattern, imag_part, cosine, precision=highest
    )
    return (out_real, out_imag)


def inner_products(left_real, left_imag, right_real, right_imag):
    over_real = jnp.einsum("mk,nk->mn", left_real, right_real, precision=highest) + jnp.einsum(
        "mk,nk->mn", left_imag, right_imag, precision=highest
    )
    over_imag = jnp.einsum("mk,nk->mn", left_real, right_imag, precision=highest) - jnp.einsum(
        "mk,nk->mn", left_imag, right_real, precision=highest
    )
    return (over_real, over_imag)


def subtract(applied_real, applied_imag, basis_real, basis_imag, weight_real, weight_imag):
    proj_real = jnp.einsum("mn,mk->nk", weight_real, basis_real, precision=highest) - jnp.einsum(
        "mn,mk->nk", weight_imag, basis_imag, precision=highest
    )
    proj_imag = jnp.einsum("mn,mk->nk", weight_imag, basis_real, precision=highest) + jnp.einsum(
        "mn,mk->nk", weight_real, basis_imag, precision=highest
    )
    return (applied_real - proj_real, applied_imag - proj_imag)


def shards(psi, potential, miller, occupied):
    grid_size = potential.shape[0]
    owners = lax.axis_size("ga")
    quarter = grid_size // 4
    per_shard = psi.shape[2]
    band_count = psi.shape[1]
    owner_index = lax.axis_index("ga")
    kept_rows = grid_size // 2
    kept_planes = grid_size // (2 * owners)
    full_index = jnp.arange(grid_size, dtype=jnp.int32)
    kept_index = (jnp.arange(kept_rows, dtype=jnp.int32) + grid_size - quarter) % grid_size
    inverse_rows = phases(kept_index, full_index, 1.0, grid_size)
    forward_rows = phases(full_index, kept_index, -1.0, grid_size)
    slot_index = jnp.arange(owners * kept_planes, dtype=jnp.int32)
    plane_index = (
        slot_index // kept_planes + owners * (slot_index % kept_planes) + grid_size - quarter
    ) % grid_size
    inverse_planes = phases(plane_index, full_index, 1.0, grid_size)
    forward_planes = phases(full_index, plane_index, -1.0, grid_size)
    local_points = lax.dynamic_slice_in_dim(miller, owner_index * per_shard, per_shard)
    index_a = local_points // (grid_size * grid_size)
    index_b = local_points // grid_size % grid_size
    index_c = local_points % grid_size
    plane_pos = (index_a + quarter) % grid_size
    position = (plane_pos // owners * kept_rows + (index_b + quarter) % grid_size) * kept_rows + (
        index_c + quarter
    ) % grid_size
    slab_size = kept_planes * kept_rows * kept_rows
    real_part = jnp.zeros((band_count, slab_size), jnp.float32).at[:, position].set(psi[0])
    imag_part = jnp.zeros((band_count, slab_size), jnp.float32).at[:, position].set(psi[1])
    real_part = real_part.reshape(band_count, kept_planes, kept_rows, kept_rows)
    imag_part = imag_part.reshape(band_count, kept_planes, kept_rows, kept_rows)
    real_part, imag_part = contract("ntbc,by->ntyc", real_part, imag_part, inverse_rows)
    pieces = (
        lax.all_to_all(real_part, "ga", split_axis=2, concat_axis=1, tiled=True),
        lax.all_to_all(imag_part, "ga", split_axis=2, concat_axis=1, tiled=True),
    )
    wide_real, wide_imag = contract("nsyc,cz->nsyz", pieces[0], pieces[1], inverse_rows)
    pieces = (wide_real, wide_imag)
    wave_real, wave_imag = contract("nsyz,sx->nxyz", pieces[0], pieces[1], inverse_planes)
    wave_real = wave_real * potential
    wave_imag = wave_imag * potential
    wide_real, wide_imag = contract("nxyz,xs->nsyz", wave_real, wave_imag, forward_planes)
    narrow = contract("nsyz,zc->nsyc", wide_real, wide_imag, forward_rows)
    real_part = lax.all_to_all(narrow[0], "ga", split_axis=1, concat_axis=2, tiled=True)
    imag_part = lax.all_to_all(narrow[1], "ga", split_axis=1, concat_axis=2, tiled=True)
    real_part, imag_part = contract("ntyc,yb->ntbc", real_part, imag_part, forward_rows)
    inverse_volume = 1.0 / grid_size**3
    applied_real = real_part.reshape(band_count, slab_size)[:, position] * inverse_volume
    applied_imag = imag_part.reshape(band_count, slab_size)[:, position] * inverse_volume
    weights = occupied.astype(jnp.float32)[:, None]
    moved_parts = (
        lax.all_to_all(applied_real, "band", split_axis=1, concat_axis=0, tiled=True),
        lax.all_to_all(applied_imag, "band", split_axis=1, concat_axis=0, tiled=True),
        lax.all_to_all(psi[0], "band", split_axis=1, concat_axis=0, tiled=True),
        lax.all_to_all(psi[1], "band", split_axis=1, concat_axis=0, tiled=True),
    )
    column_real, column_imag, basis_real, basis_imag = moved_parts
    over_real, over_imag = inner_products(basis_real, basis_imag, column_real, column_imag)
    over_real, over_imag = lax.psum((over_real, over_imag), ("ga", "band"))
    weight_real = weights * (over_real / NPW)
    weight_imag = weights * (over_imag / NPW)
    left_real, left_imag = subtract(
        column_real, column_imag, basis_real, basis_imag, weight_real, weight_imag
    )
    left_real, left_imag = (
        lax.all_to_all(left_real, "band", split_axis=0, concat_axis=1, tiled=True),
        lax.all_to_all(left_imag, "band", split_axis=0, concat_axis=1, tiled=True),
    )
    return jnp.stack([left_real, left_imag])


def solution(mesh):
    in_specs = (P(None, "band", "ga"), P("pert", "ga", None), P(), P())
    out_specs = P(None, ("pert", "band"), "ga")
    return jax.shard_map(shards, mesh=mesh, in_specs=in_specs, out_specs=out_specs, check_vma=False)
```

profile of v0, /device:TPU:0, one launch (start us, length us, event | category | flops | bytes accessed | tf_op | source)
XLA Modules:
  0.0 796.2 jit_solution(8780782208961339326)
XLA Ops:
  3.1 120.4 %scatter_custom_fusion.1 = f32[65536]{0:T(1024)S(1)} fusion(s32[32768]{0:T(1024)S(1)} %get-tuple-element.8, f32[32768]{0:T(1024)} %bitcast.7, f32[]{:T(128)} %constant.167.clone.1), kind=kCustom, calls=%fused_computation.97 | custom fusion | bytes 262656 | tf_op jit(solution)/shard_map/scatter | solution.py:76
  123.8 120.4 %scatter_custom_fusion = f32[65536]{0:T(1024)S(1)} fusion(s32[32768]{0:T(1024)S(1)} %get-tuple-element.8, f32[32768]{0:T(1024)} %bitcast.3, f32[]{:T(128)} %constant.167.clone.1), kind=kCustom, calls=%fused_computation.99 | custom fusion | bytes 262656 | tf_op jit(solution)/shard_map/scatter | solution.py:75
  248.2 6.3 all-to-all-start
  258.1 10.9 %all-to-all-done = f32[4,1,32768]{2,1,0:T(1,128)S(1)} async-done(((f32[4,1,32768]{2,1,0:T(1,128)}), f32[4,1,32768]{2,1,0:T(1,128)S(1)}, u32[]{:S(2)}, u32[]{:S(2)}) %all-to-all-start) | async-done | bytes 524320 | tf_op jit(solution)/shard_map/all_to_all | solution.py:81
  269.0 3.6 all-to-all-start.1
  278.8 7.7 all-to-all-done.1
  299.5 3.6 subtract_multiply_fusion
  306.0 3.6 add_multiply_fusion
  318.0 3.5 all-to-all-start.2
  326.5 9.0 %all-to-all-done.2 = f32[4,1,32768]{2,1,0:T(1,128)S(1)} async-done(((f32[4,1,32768]{2,1,0:T(1,128)}), f32[4,1,32768]{2,1,0:T(1,128)S(1)}, u32[]{:S(2)}, u32[]{:S(2)}) %all-to-all-start.2) | async-done | bytes 524320 | tf_op jit(solution)/shard_map/all_to_all | solution.py:91
  335.5 3.6 all-to-all-start.3
  343.7 9.4 %all-to-all-done.3 = f32[4,1,32768]{2,1,0:T(1,128)S(1)} async-done(((f32[4,1,32768]{2,1,0:T(1,128)}), f32[4,1,32768]{2,1,0:T(1,128)S(1)}, u32[]{:S(2)}, u32[]{:S(2)}) %all-to-all-start.3) | async-done | bytes 524320 | tf_op jit(solution)/shard_map/all_to_all | solution.py:92
  353.1 3.3 all-to-all-start.5
  360.3 180.5 %gather_fusion = f32[32768]{0:T(1024)S(1)} fusion(f32[65536]{0:T(1024)S(1)} %reshape.289, s32[32768]{0:T(1024)S(1)} %get-tuple-element.7), kind=kCustom, calls=%fused_computation | custom fusion | bytes 393216 | tf_op jit(solution)/shard_map/gather | solution.py:95
  542.5 180.5 %gather_fusion.1 = f32[32768]{0:T(1024)S(1)} fusion(f32[65536]{0:T(1024)S(1)} %reshape.299, s32[32768]{0:T(1024)S(1)} %get-tuple-element.7), kind=kCustom, calls=%fused_computation.1 | custom fusion | bytes 393216 | tf_op jit(solution)/shard_map/gather | solution.py:96
  723.1 3.3 all-to-all-start.4
  727.1 3.9 all-to-all-done.4
  735.0 3.9 all-to-all-done.6
  738.9 3.3 all-to-all-start.7
  742.9 3.9 all-to-all-done.7
  748.2 30.3 %all-reduce = (f32[4,4]{0,1:T(4,128)S(1)}, f32[4,4]{0,1:T(4,128)S(1)}) all-reduce(f32[4,4]{0,1:T(4,128)S(1)} %fusion.8, f32[4,4]{0,1:T(4,128)S(1)} %fusion.9), channel_id=1, replica_groups=mesh['pert'=2,'ga'=4,'band'=4] {'ga','band'}, use_global_device_ids=true, to_apply=%region_3.4 | all-reduce | flops 32 | bytes 256 | tf_op jit(solution)/shard_map/psum | solution.py:106
  780.2 3.3 all-to-all-start.8
  784.5 3.5 all-to-all-done.8
  788.1 7.0 all_to_all.144
  (75 shorter events, 66.5 us)
Async XLA Ops:
  248.2 20.8 %all-to-all-start = ((f32[4,1,32768]{2,1,0:T(1,128)}), f32[4,1,32768]{2,1,0:T(1,128)S(1)}, u32[]{:S(2)}, u32[]{:S(2)}) async-start(f32[4,1,32768]{2,1,0:T(1,128)} %reshape.365), calls=%async_computation | async-start | bytes 1048576 | tf_op jit(solution)/shard_map/all_to_all | solution.py:81
  269.0 17.5 %all-to-all-start.1 = ((f32[4,1,32768]{2,1,0:T(1,128)}), f32[4,1,32768]{2,1,0:T(1,128)S(1)}, u32[]{:S(2)}, u32[]{:S(2)}) async-start(f32[4,1,32768]{2,1,0:T(1,128)} %reshape.367), calls=%async_computation.1 | async-start | bytes 1048576 | tf_op jit(solution)/shard_map/all_to_all | solution.py:82
  297.9 1.6 copy-start
  318.0 17.5 %all-to-all-start.2 = ((f32[4,1,32768]{2,1,0:T(1,128)}), f32[4,1,32768]{2,1,0:T(1,128)S(1)}, u32[]{:S(2)}, u32[]{:S(2)}) async-start(f32[4,1,32768]{2,1,0:T(1,128)} %reshape.369), calls=%async_computation.2 | async-start | bytes 1048576 | tf_op jit(solution)/shard_map/all_to_all | solution.py:91
  335.5 17.6 %all-to-all-start.3 = ((f32[4,1,32768]{2,1,0:T(1,128)}), f32[4,1,32768]{2,1,0:T(1,128)S(1)}, u32[]{:S(2)}, u32[]{:S(2)}) async-start(f32[4,1,32768]{2,1,0:T(1,128)} %reshape.371), calls=%async_computation.3 | async-start | bytes 1048576 | tf_op jit(solution)/shard_map/all_to_all | solution.py:92
  353.1 370.0 %all-to-all-start.5 = ((f32[1,4,8192]{2,0,1:T(1,128)}), f32[1,4,8192]{2,0,1:T(1,128)S(1)}, u32[]{:S(2)}, u32[]{:S(2)}) async-start(f32[1,4,8192]{2,0,1:T(1,128)} %bitcast.45), calls=%async_computation.5 | async-start | bytes 262144 | tf_op jit(solution)/shard_map/all_to_all | solution.py:101
  723.0 25.2 %copy-start.1 = (s32[4]{0:T(128)S(1)}, s32[4]{0:T(128)}, u32[]{:S(2)}) copy-start(s32[4]{0:T(128)} %param.7) | copy-start | bytes 52
  723.1 7.9 all-to-all-start.4
  731.0 7.9 all-to-all-start.6
  738.9 7.9 all-to-all-start.7
  780.2 7.9 all-to-all-start.8
where the time goes:
time: 803 us; the launch traced here: 796 us
  local copies, waits for them, and re-layouts  617 us (77%)
  waiting for transfers between devices  52.2 us (7%)
  matrix products  41.5 us (5%)
  blocking collectives  37.2 us (5%)
  starting transfers between devices  33.7 us (4%)
  other arithmetic  13.3 us (2%)
    gather x1, local copies, waits for them, and re-layouts, shards(): real_part.reshape(band_count, slab_size)[:, position] * inverse_volume  181 us
    gather x1, local copies, waits for them, and re-layouts, shards(): imag_part.reshape(band_count, slab_size)[:, position] * inverse_volume  181 us
    scatter x1, local copies, waits for them, and re-layouts, shards(): jnp.zeros((band_count, slab_size), jnp.float32).at[:, position].set(psi[0])  120 us
    scatter x1, local copies, waits for them, and re-layouts, shards(): jnp.zeros((band_count, slab_size), jnp.float32).at[:, position].set(psi[1])  120 us
    psum x1, blocking collectives, shards(): over_real, over_imag = lax.psum((over_real, over_imag), ('ga', 'band'))  30.3 us
  transfers between devices with their start and end apart: 9, of which 8 were waited for; matrix products, arithmetic and copies ran while one was open for 49% of the time, Pallas kernels for 0%

commit v1 on v0

--- a/solution.py
+++ b/solution.py
@@ -1,3 +1,4 @@
+import functools
 import jax
 import jax.numpy as jnp
 from jax import lax
@@ -5,6 +6,22 @@
 
 NPW = 131072
 highest = lax.Precision.HIGHEST
+
+
+def ports_report(w_in, bus_axis, row_dim, dimension_no):
+    u1 = jnp.concatenate(
+        lax.all_to_all(
+            jnp.stack(jnp.split(w_in, lax.axis_size(bus_axis), axis=row_dim), axis=0),
+            bus_axis,
+            0,
+            0,
+        ),
+        axis=dimension_no,
+    )
+    return u1
+
+
+positions_extend = functools.partial(ports_report, bus_axis="ga", row_dim=2, dimension_no=1)
 
 
 def phases(first_index, second_index, direction, length):
@@ -78,7 +95,7 @@
     imag_part = imag_part.reshape(band_count, kept_planes, kept_rows, kept_rows)
     real_part, imag_part = contract("ntbc,by->ntyc", real_part, imag_part, inverse_rows)
     pieces = (
-        lax.all_to_all(real_part, "ga", split_axis=2, concat_axis=1, tiled=True),
+        positions_extend(real_part),
         lax.all_to_all(imag_part, "ga", split_axis=2, concat_axis=1, tiled=True),
     )
     wide_real, wide_imag = contract("nsyc,cz->nsyz", pieces[0], pieces[1], inverse_rows)

time: 803 us -> 808 us (level)
  transfers between devices with their start and end apart: 9 -> 9, of which waited for: 8 -> 8; matrix products, arithmetic and copies ran while one was open for 49% -> 48% of each run, Pallas kernels for 0% -> 0%
where the time goes in v1:
time: 808 us; the launch traced here: 801 us
  local copies, waits for them, and re-layouts  620 us (77%)
  waiting for transfers between devices  52.9 us (7%)
  matrix products  41.5 us (5%)
  blocking collectives  37.2 us (5%)
  starting transfers between devices  34.4 us (4%)
  other arithmetic  14.2 us (2%)
    gather x1, local copies, waits for them, and re-layouts, shards(): imag_part.reshape(band_count, slab_size)[:, position] * inverse_volume  181 us
    gather x1, local copies, waits for them, and re-layouts, shards(): real_part.reshape(band_count, slab_size)[:, position] * inverse_volume  181 us
    scatter x1, local copies, waits for them, and re-layouts, shards(): jnp.zeros((band_count, slab_size), jnp.float32).at[:, position].set(psi[0])  120 us
    scatter x1, local copies, waits for them, and re-layouts, shards(): jnp.zeros((band_count, slab_size), jnp.float32).at[:, position].set(psi[1])  120 us
    psum x1, blocking collectives, shards(): over_real, over_imag = lax.psum((over_real, over_imag), ('ga', 'band'))  30.3 us
  transfers between devices with their start and end apart: 9, of which 8 were waited for; matrix products, arithmetic and copies ran while one was open for 48% of the time, Pallas kernels for 0%

profile of v1, /device:TPU:0, one launch (start us, length us, event | category | flops | bytes accessed | tf_op | source)
XLA Modules:
  0.0 800.8 jit_solution(4541529143578964517)
XLA Ops:
  3.1 120.4 %scatter_custom_fusion.1 = f32[65536]{0:T(1024)S(1)} fusion(s32[32768]{0:T(1024)S(1)} %get-tuple-element.8, f32[32768]{0:T(1024)} %bitcast.7, f32[]{:T(128)} %constant.167.clone.1), kind=kCustom, calls=%fused_computation.102 | custom fusion | bytes 262656 | tf_op jit(solution)/shard_map/scatter | solution.py:93
  123.8 120.4 %scatter_custom_fusion = f32[65536]{0:T(1024)S(1)} fusion(s32[32768]{0:T(1024)S(1)} %get-tuple-element.8, f32[32768]{0:T(1024)} %bitcast.3, f32[]{:T(128)} %constant.167.clone.1), kind=kCustom, calls=%fused_computation.104 | custom fusion | bytes 262656 | tf_op jit(solution)/shard_map/scatter | solution.py:92
  251.2 6.4 all-to-all-start
  261.1 10.9 %all-to-all-done = f32[4,1,32768]{2,1,0:T(1,128)S(1)} async-done(((f32[4,1,32768]{2,1,0:T(1,128)}), f32[4,1,32768]{2,1,0:T(1,128)S(1)}, u32[]{:S(2)}, u32[]{:S(2)}) %all-to-all-start) | async-done | bytes 524320 | tf_op jit(solution)/shard_map/all_to_all | solution.py:13
  272.1 4.3 all-to-all-start.1
  282.0 8.4 %all-to-all-done.1 = f32[4,1,32768]{2,1,0:T(1,128)} async-done(((f32[4,1,32768]{2,1,0:T(1,128)}), f32[4,1,32768]{2,1,0:T(1,128)}, u32[]{:S(2)}, u32[]{:S(2)}) %all-to-all-start.1) | async-done | bytes 524320 | tf_op jit(solution)/shard_map/all_to_all | solution.py:99
  290.3 3.8 reduce.1
  304.2 3.6 subtract_multiply_fusion
  310.7 3.6 add_multiply_fusion
  322.6 3.5 all-to-all-start.2
  331.1 9.0 %all-to-all-done.2 = f32[4,1,32768]{2,1,0:T(1,128)S(1)} async-done(((f32[4,1,32768]{2,1,0:T(1,128)}), f32[4,1,32768]{2,1,0:T(1,128)S(1)}, u32[]{:S(2)}, u32[]{:S(2)}) %all-to-all-start.2) | async-done | bytes 524320 | tf_op jit(solution)/shard_map/all_to_all | solution.py:108
  340.1 3.6 all-to-all-start.3
  348.2 9.5 %all-to-all-done.3 = f32[4,1,32768]{2,1,0:T(1,128)S(1)} async-done(((f32[4,1,32768]{2,1,0:T(1,128)}), f32[4,1,32768]{2,1,0:T(1,128)S(1)}, u32[]{:S(2)}, u32[]{:S(2)}) %all-to-all-start.3) | async-done | bytes 524320 | tf_op jit(solution)/shard_map/all_to_all | solution.py:109
  364.8 180.5 %gather_fusion = f32[32768]{0:T(1024)S(1)} fusion(f32[65536]{0:T(1024)S(1)} %reshape.290, s32[32768]{0:T(1024)S(1)} %get-tuple-element.7), kind=kCustom, calls=%fused_computation | custom fusion | bytes 393216 | tf_op jit(solution)/shard_map/gather | solution.py:112
  547.1 180.5 %gather_fusion.1 = f32[32768]{0:T(1024)S(1)} fusion(f32[65536]{0:T(1024)S(1)} %reshape.300, s32[32768]{0:T(1024)S(1)} %get-tuple-element.7), kind=kCustom, calls=%fused_computation.1 | custom fusion | bytes 393216 | tf_op jit(solution)/shard_map/gather | solution.py:113
  727.6 3.3 all-to-all-start.4
  731.6 3.9 all-to-all-done.4
  739.6 3.9 all-to-all-done.6
  743.4 3.3 all-to-all-start.7
  747.5 3.9 all-to-all-done.7
  752.8 30.3 %all-reduce = (f32[4,4]{0,1:T(4,128)S(1)}, f32[4,4]{0,1:T(4,128)S(1)}) all-reduce(f32[4,4]{0,1:T(4,128)S(1)} %fusion.8, f32[4,4]{0,1:T(4,128)S(1)} %fusion.9), channel_id=1, replica_groups=mesh['pert'=2,'ga'=4,'band'=4] {'ga','band'}, use_global_device_ids=true, to_apply=%region_3.4 | all-reduce | flops 32 | bytes 256 | tf_op jit(solution)/shard_map/psum | solution.py:123
  784.8 3.3 all-to-all-start.8
  789.1 3.5 all-to-all-done.8
  792.7 7.0 all_to_all.134
  (75 shorter events, 69.2 us)
Async XLA Ops:
  251.2 20.8 %all-to-all-start = ((f32[4,1,32768]{2,1,0:T(1,128)}), f32[4,1,32768]{2,1,0:T(1,128)S(1)}, u32[]{:S(2)}, u32[]{:S(2)}) async-start(f32[4,1,32768]{2,1,0:T(1,128)} %reshape.366), calls=%async_computation | async-start | bytes 1048576 | tf_op jit(solution)/shard_map/all_to_all | solution.py:13
  272.1 18.3 %all-to-all-start.1 = ((f32[4,1,32768]{2,1,0:T(1,128)}), f32[4,1,32768]{2,1,0:T(1,128)}, u32[]{:S(2)}, u32[]{:S(2)}) async-start(f32[4,1,32768]{2,1,0:T(1,128)} %reshape.368), calls=%async_computation.1 | async-start | bytes 1048576 | tf_op jit(solution)/shard_map/all_to_all | solution.py:99
  302.6 1.6 copy-start
  322.6 17.5 %all-to-all-start.2 = ((f32[4,1,32768]{2,1,0:T(1,128)}), f32[4,1,32768]{2,1,0:T(1,128)S(1)}, u32[]{:S(2)}, u32[]{:S(2)}) async-start(f32[4,1,32768]{2,1,0:T(1,128)} %reshape.370), calls=%async_computation.2 | async-start | bytes 1048576 | tf_op jit(solution)/shard_map/all_to_all | solution.py:108
  340.1 17.6 %all-to-all-start.3 = ((f32[4,1,32768]{2,1,0:T(1,128)}), f32[4,1,32768]{2,1,0:T(1,128)S(1)}, u32[]{:S(2)}, u32[]{:S(2)}) async-start(f32[4,1,32768]{2,1,0:T(1,128)} %reshape.372), calls=%async_computation.3 | async-start | bytes 1048576 | tf_op jit(solution)/shard_map/all_to_all | solution.py:109
  357.7 369.9 %all-to-all-start.5 = ((f32[1,4,8192]{2,0,1:T(1,128)}), f32[1,4,8192]{2,0,1:T(1,128)S(1)}, u32[]{:S(2)}, u32[]{:S(2)}) async-start(f32[1,4,8192]{2,0,1:T(1,128)} %bitcast.48), calls=%async_computation.5 | async-start | bytes 262144 | tf_op jit(solution)/shard_map/all_to_all | solution.py:118
  727.6 25.2 %copy-start.1 = (s32[4]{0:T(128)S(1)}, s32[4]{0:T(128)}, u32[]{:S(2)}) copy-start(s32[4]{0:T(128)} %param.7) | copy-start | bytes 52
  727.6 7.9 all-to-all-start.4
  735.5 7.9 all-to-all-start.6
  743.4 7.9 all-to-all-start.7
  784.8 7.9 all-to-all-start.8
